TPU v7x, 512 devices: a whole 4x8x8 slice. The times are simulated.
512 devices in a mesh: dp: 32 (over z, x), rows: 16 (over y, core).
Axes of the slice: x: 4, y: 8, z: 8, core: 2. Of those that a mesh axis runs over, the one named last changes fastest.
Arguments:
- older_output: bfloat16 [7680, 12, 2048], P(('dp', 'rows')), parts along dimension 0, may hold values from -6 to 6
- newer_output: bfloat16 [7680, 12, 2048], P(('dp', 'rows')), parts along dimension 0, may hold values from -6 to 6
- output_grad: bfloat16 [7680, 12, 2048], P(('dp', 'rows')), parts along dimension 0, may hold values from -6 to 6
- older_weight: bfloat16 [2048, 512], P('rows'), may hold values from -0.1875 to 0.1875
- newer_weight: bfloat16 [2048, 512], P('rows'), may hold values from -0.1875 to 0.1875
- square_point: bfloat16 [512, 512], P('rows'), may hold values from -0.25 to 0.25
- column_point: bfloat16 [512, 512], P('rows'), may hold values from -0.25 to 0.25
- square_kernel: float32 [3, 3, 512], replicated, may hold values from -2.4 to 2.4
- column_kernel: float32 [7, 512], replicated, may hold values from -2.4 to 2.4
Outputs:
- cell_output: bfloat16 [7680, 12, 2048], P(('dp', 'rows')), parts along dimension 0
- older_grad: bfloat16 [7680, 12, 2048], P(('dp', 'rows')), parts along dimension 0
- newer_grad: bfloat16 [7680, 12, 2048], P(('dp', 'rows')), parts along dimension 0
There are 32 independent parts, one for each index of `dp`. A program takes and returns all parts, laid end to end along the dimension named above; an argument that names none is the same for every part. Nothing has to cross between parts.
All inputs are finite; a program needn't handle non-finite values.
Results may differ from a plain program's by a relative error of at most 0.0057.
Values may be sent and summed in bfloat16 or wider, within the bound.
No kernel may reach another device: no remote copies, remote signals or barrier semaphores. Data moves between devices by JAX's collectives and lax.ppermute only.
A program may use at most 64 MiB of HBM per device.

v0:
```python
import jax
import jax.numpy as jnp
from jax import lax
from jax.sharding import PartitionSpec as P

HEIGHT = 30


def with_halo(block, sides, width):
    for axis, dim in sides:
        count = lax.axis_size(axis)
        forward = [(i, i + 1) for i in range(count - 1)]
        backward = [(target, source) for source, target in forward]
        low = lax.ppermute(
            lax.slice_in_dim(block, block.shape[dim] - width, None, axis=dim), axis, forward
        )
        high = lax.ppermute(lax.slice_in_dim(block, 0, width, axis=dim), axis, backward)
        block = jnp.concatenate([low, block, high], axis=dim)
    return block


def same_image(first_row, local_rows, offset):
    row_ids = jnp.arange(local_rows, dtype=jnp.int32) + first_row
    inside = jnp.floor_divide(row_ids + offset, HEIGHT) == jnp.floor_divide(row_ids, HEIGHT)
    return jnp.where(inside, 1.0, 0.0).astype(jnp.float32)[:, None, None]


def square_taps(padded, kernel, flip, first_row):
    full = jnp.pad(padded, ((0, 0), (1, 1), (0, 0))).astype(jnp.float32)
    height = full.shape[0] - 2
    across = full.shape[1] - 2
    total = jnp.zeros((height, across, full.shape[2]), jnp.float32)
    for i in range(3):
        keep = same_image(first_row, height, (2 - i if flip else i) - 1)
        for j in range(3):
            first = 2 - i if flip else i
            second = 2 - j if flip else j
            total = total + full[first : first + height, second : second + across, :] * (
                kernel[i, j] * keep
            )
    return total


def column_taps(padded, kernel, flip, first_row):
    full = padded.astype(jnp.float32)
    height = full.shape[0] - 6
    total = jnp.zeros((height, full.shape[1], full.shape[2]), jnp.float32)
    for i in range(7):
        first = 6 - i if flip else i
        keep = same_image(first_row, height, first - 3)
        total = total + full[first : first + height, :, :] * (kernel[i] * keep)
    return total


def local(
    older_output,
    newer_output,
    output_grad,
    older_weight,
    newer_weight,
    square_point,
    column_point,
    square_kernel,
    column_kernel,
):
    height, across, channels = older_output.shape
    filters = square_point.shape[1]
    shape_three = (height, across, filters)
    first_row = lax.axis_index("rows") * height
    pool_kernel = jnp.full((3, 3, filters), 1.0 / 9.0, jnp.float32)
    older_flat = older_output.reshape(-1, channels)
    newer_flat = newer_output.reshape(-1, channels)
    older_relu = jnp.maximum(older_flat, 0)
    newer_relu = jnp.maximum(newer_flat, 0)
    older_full, newer_full = (
        lax.all_gather(older_weight, "rows", axis=0, tiled=True),
        lax.all_gather(newer_weight, "rows", axis=0, tiled=True),
    )
    older_sum = jnp.dot(older_relu, older_full, preferred_element_type=jnp.float32)
    newer_sum = jnp.dot(newer_relu, newer_full, preferred_element_type=jnp.float32)
    older_mixed = older_sum.astype(jnp.bfloat16).reshape(shape_three)
    newer_mixed = newer_sum.astype(jnp.bfloat16).reshape(shape_three)
    square_full, column_full = (
        lax.all_gather(square_point, "rows", axis=0, tiled=True),
        lax.all_gather(column_point, "rows", axis=0, tiled=True),
    )
    older_rim = with_halo(older_mixed, (("rows", 0),), 3)
    newer_rim = with_halo(newer_mixed, (("rows", 0),), 1)
    square_pre = (
        square_taps(newer_rim, square_kernel, False, first_row)
        .astype(jnp.bfloat16)
        .reshape(-1, filters)
    )
    column_pre = (
        column_taps(older_rim, column_kernel, False, first_row)
        .astype(jnp.bfloat16)
        .reshape(-1, filters)
    )
    pooled = square_taps(older_rim[2:-2], pool_kernel, False, first_row).reshape(-1, filters)
    square_branch = jnp.dot(square_pre, square_full, preferred_element_type=jnp.float32)
    column_branch = jnp.dot(column_pre, column_full, preferred_element_type=jnp.float32)
    cell_output = jnp.concatenate(
        [
            square_branch,
            column_branch,
            pooled,
            newer_mixed.reshape(-1, filters).astype(jnp.float32),
        ],
        axis=1,
    )
    cell_output = cell_output.astype(jnp.bfloat16).reshape(height, across, 4 * filters)
    grads = output_grad.reshape(-1, 4 * filters)
    grad_square = grads[:, :filters]
    grad_column = grads[:, filters : 2 * filters]
    grad_pool = grads[:, 2 * filters : 3 * filters].reshape(shape_three)
    grad_same = grads[:, 3 * filters :].reshape(shape_three)
    square_back = (
        jnp.dot(grad_square, square_full.T, preferred_element_type=jnp.float32)
        .astype(jnp.bfloat16)
        .reshape(shape_three)
    )
    column_back = (
        jnp.dot(grad_column, column_full.T, preferred_element_type=jnp.float32)
        .astype(jnp.bfloat16)
        .reshape(shape_three)
    )
    column_rim = with_halo(column_back, (("rows", 0),), 3)
    square_rim, pool_rim = (
        with_halo(square_back, (("rows", 0),), 1),
        with_halo(grad_pool, (("rows", 0),), 1),
    )
    newer_back = (
        (square_taps(square_rim, square_kernel, True, first_row) + grad_same.astype(jnp.float32))
        .astype(jnp.bfloat16)
        .reshape(-1, filters)
    )
    older_back = (
        (
            column_taps(column_rim, column_kernel, True, first_row)
            + square_taps(pool_rim, pool_kernel, True, first_row)
        )
        .astype(jnp.bfloat16)
        .reshape(-1, filters)
    )
    older_mask = jnp.where(older_flat > 0, 1.0, 0.0).astype(jnp.float32)
    newer_mask = jnp.where(newer_flat > 0, 1.0, 0.0).astype(jnp.float32)
    older_term = jnp.dot(older_back, older_full.T, preferred_element_type=jnp.float32)
    newer_term = jnp.dot(newer_back, newer_full.T, preferred_element_type=jnp.float32)
    older_grad = (older_term * older_mask).astype(jnp.bfloat16).reshape(older_output.shape)
    newer_grad = (newer_term * newer_mask).astype(jnp.bfloat16).reshape(newer_output.shape)
    return (cell_output, older_grad, newer_grad)


def solution(mesh):
    in_specs = (
        P(("dp", "rows"), None, None),
        P(("dp", "rows"), None, None),
        P(("dp", "rows"), None, None),
        P("rows", None),
        P("rows", None),
        P("rows", None),
        P("rows", None),
        P(),
        P(),
    )
    out_specs = (
        P(("dp", "rows"), None, None),
        P(("dp", "rows"), None, None),
        P(("dp", "rows"), None, None),
    )
    return jax.shard_map(local, mesh=mesh, in_specs=in_specs, out_specs=out_specs, check_vma=False)
```

profile of v0, /device:TPU:1, one launch (start us, length us, event | category | flops | bytes accessed | tf_op | source)
XLA Modules:
  0.0 140.9 jit_solution(8323920743990531332)
XLA Ops:
  8.0 1.6 %copy.52 = bf16[15,12,2048]{2,1,0:T(8,128)(2,1)S(1)} copy(bf16[15,12,2048]{2,0,1:T(8,128)(2,1)} %param.11) | data formatting | bytes 1474560 | tf_op args[2]
  9.7 22.4 %all_gather.13 = bf16[512,512]{1,0:T(8,128)(2,1)S(1)} all-gather(bf16[32,512]{1,0:T(8,128)(2,1)S(1)} %copy-done.40), channel_id=1, replica_groups=mesh['dp'=32,'rows'=16] {'rows'}, dimensions={0}, use_global_device_ids=true | all-gather | bytes 557056 | tf_op jit(solution)/shard_map/all_gather | solution.py:84
  34.0 3.7 %collective-permute-start.8 = (bf16[1,12,512]{2,1,0:T(8,128)(2,1)}, bf16[1,12,512]{2,1,0:T(8,128)(2,1)}, u32[]{:S(2)}, u32[]{:S(2)}) collective-permute-start(bf16[1,12,512]{2,1,0:T(8,128)(2,1)} %get-tuple-element.18), channel_id=1, source_target_pairs={{0,1},{1,2},{2,3},{3,4},{4,5},{5,6},{6,7},{7,8},{8,9},{9,10},{10,1... | collective-permute-start | bytes 36872 | tf_op jit(solution)/shard_map/ppermute | solution.py:14
  37.7 1.9 %collective-permute-start.9 = (bf16[1,12,512]{2,1,0:T(8,128)(2,1)}, bf16[1,12,512]{2,1,0:T(8,128)(2,1)}, u32[]{:S(2)}, u32[]{:S(2)}) collective-permute-start(bf16[1,12,512]{2,1,0:T(8,128)(2,1)} %get-tuple-element.19), channel_id=1, source_target_pairs={{1,0},{2,1},{3,2},{4,3},{5,4},{6,5},{7,6},{8,7},{9,8},{10,9},{11,1... | collective-permute-start | bytes 36872 | tf_op jit(solution)/shard_map/ppermute | solution.py:17
  40.3 1.9 %collective-permute-start.7 = (bf16[1,12,512]{2,0,1:T(2,128)(2,1)}, bf16[1,12,512]{2,0,1:T(2,128)(2,1)}, u32[]{:S(2)}, u32[]{:S(2)}) collective-permute-start(bf16[1,12,512]{2,0,1:T(2,128)(2,1)} %copy.57), channel_id=1, source_target_pairs={{1,0},{2,1},{3,2},{4,3},{5,4},{6,5},{7,6},{8,7},{9,8},{10,9},{11,1... | collective-permute-start | bytes 36872 | tf_op jit(solution)/shard_map/ppermute | solution.py:17
  42.8 3.6 %collective-permute-start.6 = (bf16[1,12,512]{2,0,1:T(2,128)(2,1)}, bf16[1,12,512]{2,0,1:T(2,128)(2,1)}, u32[]{:S(2)}, u32[]{:S(2)}) collective-permute-start(bf16[1,12,512]{2,0,1:T(2,128)(2,1)} %copy.56), channel_id=1, source_target_pairs={{0,1},{1,2},{2,3},{3,4},{4,5},{5,6},{6,7},{7,8},{8,9},{9,10},{10,1... | collective-permute-start | bytes 36872 | tf_op jit(solution)/shard_map/ppermute | solution.py:14
  46.4 17.1 %all_gather.15 = bf16[512,512]{1,0:T(8,128)(2,1)S(1)} all-gather(bf16[32,512]{1,0:T(8,128)(2,1)S(1)} %copy-done.41), channel_id=1, replica_groups=mesh['dp'=32,'rows'=16] {'rows'}, dimensions={0}, use_global_device_ids=true | all-gather | bytes 557056 | tf_op jit(solution)/shard_map/all_gather | solution.py:85
  65.9 2.1 %collective-permute-start.5 = (bf16[3,12,512]{2,0,1:T(4,128)(2,1)}, bf16[3,12,512]{2,0,1:T(4,128)(2,1)}, u32[]{:S(2)}, u32[]{:S(2)}) collective-permute-start(bf16[3,12,512]{2,0,1:T(4,128)(2,1)} %copy.54), channel_id=1, source_target_pairs={{1,0},{2,1},{3,2},{4,3},{5,4},{6,5},{7,6},{8,7},{9,8},{10,9},{11,1... | collective-permute-start | bytes 110600 | tf_op jit(solution)/shard_map/ppermute | solution.py:17
  72.4 1.3 compare_select_fusion.1
  76.1 1.6 %copy.47 = bf16[15,12,2048]{2,1,0:T(8,128)(2,1)S(1)} copy(bf16[15,12,2048]{2,0,1:T(8,128)(2,1)} %broadcast_maximum_fusion) | data formatting | bytes 1474560 | tf_op jit(solution)/shard_map/max | solution.py:73
  83.4 2.3 %copy.60 = f32[15,12,2048]{2,1,0:T(8,128)S(1)} copy(f32[15,12,2048]{2,0,1:T(8,128)} %compare_select_fusion.1) | data formatting | bytes 2949120 | tf_op jit(solution)/shard_map/jit(_where)/select_n | solution.py:145
  85.7 1.4 select_n.201
  88.0 1.3 select_n.203
  89.3 3.5 %collective-permute-start.4 = (bf16[3,12,512]{2,0,1:T(4,128)(2,1)S(1)}, bf16[3,12,512]{2,0,1:T(4,128)(2,1)S(1)}, u32[]{:S(2)}, u32[]{:S(2)}) collective-permute-start(bf16[3,12,512]{2,0,1:T(4,128)(2,1)S(1)} %copy-done.39), channel_id=1, source_target_pairs={{0,1},{1,2},{2,3},{3,4},{4,5},{5,6},{6,7},{7,8},{8,9},{9,10},{10,1... | collective-permute-start | bytes 110600 | tf_op jit(solution)/shard_map/ppermute | solution.py:14
  98.1 2.2 %convolution_convert_fusion.4 = bf16[180,512]{1,0:T(8,128)(2,1)S(1)} fusion(bf16[180,2048]{1,0:T(8,128)(2,1)S(1)} %copy-done.8, bf16[2048,512]{1,0:T(8,128)(2,1)} %all-gather.5.cloned.1.call-done), kind=kOutput, calls=%fused_computation.10 | convolution fusion | flops 377579520 | bytes 3018752 | tf_op jit(solution)/shard_map/dot_general | solution.py:79
  100.5 2.1 %collective-permute-start.3 = (bf16[3,12,512]{2,0,1:T(4,128)(2,1)S(1)}, bf16[3,12,512]{2,0,1:T(4,128)(2,1)S(1)}, u32[]{:S(2)}, u32[]{:S(2)}) collective-permute-start(bf16[3,12,512]{2,0,1:T(4,128)(2,1)S(1)} %copy.49), channel_id=1, source_target_pairs={{1,0},{2,1},{3,2},{4,3},{5,4},{6,5},{7,6},{8,7},{9,8},{10,9},{11,1... | collective-permute-start | bytes 110600 | tf_op jit(solution)/shard_map/ppermute | solution.py:17
  102.5 7.8 %all-gather.3.cloned.1.call-done = bf16[2048,512]{1,0:T(8,128)(2,1)} async-done(((bf16[128,512]{1,0:T(8,128)(2,1)}), bf16[2048,512]{1,0:T(8,128)(2,1)}) %all-gather.3.cloned.1.call-update) | async-done | bytes 2097168 | tf_op jit(solution)/shard_map/all_gather | solution.py:77
  110.3 2.1 %convolution_convert_fusion.5 = bf16[180,512]{1,0:T(8,128)(2,1)S(1)} fusion(bf16[180,2048]{1,0:T(8,128)(2,1)S(1)} %copy-done.7, bf16[2048,512]{1,0:T(8,128)(2,1)} %all-gather.3.cloned.1.call-done), kind=kOutput, calls=%fused_computation.11 | convolution fusion | flops 377579520 | bytes 3018752 | tf_op jit(solution)/shard_map/dot_general | solution.py:80
  113.1 2.9 %collective-permute-start = (bf16[1,12,512]{2,1,0:T(8,128)(2,1)}, bf16[1,12,512]{2,1,0:T(8,128)(2,1)}, u32[]{:S(2)}, u32[]{:S(2)}) collective-permute-start(bf16[1,12,512]{2,1,0:T(8,128)(2,1)} %get-tuple-element.22), channel_id=1, source_target_pairs={{0,1},{1,2},{2,3},{3,4},{4,5},{5,6},{6,7},{7,8},{8,9},{9,10},{10,1... | collective-permute-start | bytes 36872 | tf_op jit(solution)/shard_map/ppermute | solution.py:14
  116.0 2.2 %collective-permute-start.1 = (bf16[1,12,512]{2,1,0:T(8,128)(2,1)}, bf16[1,12,512]{2,1,0:T(8,128)(2,1)}, u32[]{:S(2)}, u32[]{:S(2)}) collective-permute-start(bf16[1,12,512]{2,1,0:T(8,128)(2,1)} %get-tuple-element.23), channel_id=1, source_target_pairs={{1,0},{2,1},{3,2},{4,3},{5,4},{6,5},{7,6},{8,7},{9,8},{10,9},{11,1... | collective-permute-start | bytes 36872 | tf_op jit(solution)/shard_map/ppermute | solution.py:17
  118.3 2.3 %fusion = bf16[180,2048]{1,0:T(8,128)(2,1)S(1)} fusion(f32[180,2048]{1,0:T(8,128)} %select_n.201, bf16[180,512]{1,0:T(8,128)(2,1)} %reshape.949, bf16[2048,512]{1,0:T(8,128)(2,1)S(1)} %copy-done), kind=kOutput, calls=%fused_computation.2 | convolution fusion | flops 378224640 | bytes 4493312 | tf_op jit(solution)/shard_map/dot_general | solution.py:147
  121.8 3.8 %collective-permute-start.2 = (bf16[3,12,512]{2,0,1:T(4,128)(2,1)S(1)}, bf16[3,12,512]{2,0,1:T(4,128)(2,1)S(1)}, u32[]{:S(2)}, u32[]{:S(2)}) collective-permute-start(bf16[3,12,512]{2,0,1:T(4,128)(2,1)S(1)} %copy.48), channel_id=1, source_target_pairs={{0,1},{1,2},{2,3},{3,4},{4,5},{5,6},{6,7},{7,8},{8,9},{9,10},{10,1... | collective-permute-start | bytes 110600 | tf_op jit(solution)/shard_map/ppermute | solution.py:14
  125.9 1.3 copy.62
  127.4 1.3 copy.63
  (204 shorter events, 32.0 us)
Async XLA Ops:
  7.2 91.0 %all-gather.5.cloned.1.call-start = ((), (), s32[]{:S(2)}) async-start(), calls=%async_computation.1 | async-start | bytes 2228224 | tf_op jit(solution)/shard_map/all_gather | solution.py:76
  7.9 102.4 %all-gather.3.cloned.1.call-start = ((), (), s32[]{:S(2)}) async-start(), calls=%async_computation | async-start | bytes 2228224 | tf_op jit(solution)/shard_map/all_gather | solution.py:77
  9.5 36.9 %copy-start.41 = (bf16[32,512]{1,0:T(8,128)(2,1)S(1)}, bf16[32,512]{1,0:T(8,128)(2,1)}, u32[]{:S(2)}) copy-start(bf16[32,512]{1,0:T(8,128)(2,1)} %param.15) | copy-start | bytes 98308
  33.0 35.1 %copy-start.55 = (f32[7,512]{1,0:T(8,128)S(1)}, f32[7,512]{1,0:T(8,128)}, u32[]{:S(2)}) copy-start(f32[7,512]{1,0:T(8,128)} %param.17) | copy-start | bytes 43012
  33.0 35.1 %copy-start.54 = (f32[3,3,512]{2,1,0:T(4,128)S(1)}, f32[3,3,512]{2,1,0:T(4,128)}, u32[]{:S(2)}) copy-start(f32[3,3,512]{2,1,0:T(4,128)} %param.16) | copy-start | bytes 55300
  33.3 31.3 %copy-start.15 = (bf16[180,512]{1,0:T(8,128)(2,1)}, bf16[180,512]{1,0:T(8,128)(2,1)S(1)}, u32[]{:S(2)}) copy-start(bf16[180,512]{1,0:T(8,128)(2,1)S(1)} %convolution_convert_fusion.2) | copy-start | bytes 552964
  34.0 55.3 %collective-permute-start.8 = (bf16[1,12,512]{2,1,0:T(8,128)(2,1)}, bf16[1,12,512]{2,1,0:T(8,128)(2,1)}, u32[]{:S(2)}, u32[]{:S(2)}) collective-permute-start(bf16[1,12,512]{2,1,0:T(8,128)(2,1)} %get-tuple-element.18), channel_id=1, source_target_pairs={{0,1},{1,2},{2,3},{3,4},{4,5},{5,6},{6,7},{7,8},{8,9},{9,10},{10,1... | collective-permute-start | bytes 36872 | tf_op jit(solution)/shard_map/ppermute | solution.py:14
  37.7 55.1 %collective-permute-start.9 = (bf16[1,12,512]{2,1,0:T(8,128)(2,1)}, bf16[1,12,512]{2,1,0:T(8,128)(2,1)}, u32[]{:S(2)}, u32[]{:S(2)}) collective-permute-start(bf16[1,12,512]{2,1,0:T(8,128)(2,1)} %get-tuple-element.19), channel_id=1, source_target_pairs={{1,0},{2,1},{3,2},{4,3},{5,4},{6,5},{7,6},{8,7},{9,8},{10,9},{11,1... | collective-permute-start | bytes 36872 | tf_op jit(solution)/shard_map/ppermute | solution.py:17
  40.3 54.0 %collective-permute-start.7 = (bf16[1,12,512]{2,0,1:T(2,128)(2,1)}, bf16[1,12,512]{2,0,1:T(2,128)(2,1)}, u32[]{:S(2)}, u32[]{:S(2)}) collective-permute-start(bf16[1,12,512]{2,0,1:T(2,128)(2,1)} %copy.57), channel_id=1, source_target_pairs={{1,0},{2,1},{3,2},{4,3},{5,4},{6,5},{7,6},{8,7},{9,8},{10,9},{11,1... | collective-permute-start | bytes 36872 | tf_op jit(solution)/shard_map/ppermute | solution.py:17
  42.8 51.5 %collective-permute-start.6 = (bf16[1,12,512]{2,0,1:T(2,128)(2,1)}, bf16[1,12,512]{2,0,1:T(2,128)(2,1)}, u32[]{:S(2)}, u32[]{:S(2)}) collective-permute-start(bf16[1,12,512]{2,0,1:T(2,128)(2,1)} %copy.56), channel_id=1, source_target_pairs={{0,1},{1,2},{2,3},{3,4},{4,5},{5,6},{6,7},{7,8},{8,9},{9,10},{10,1... | collective-permute-start | bytes 36872 | tf_op jit(solution)/shard_map/ppermute | solution.py:14
  64.3 7.1 %copy-start.5 = (bf16[15,12,2048]{2,0,1:T(8,128)(2,1)S(1)}, bf16[15,12,2048]{2,0,1:T(8,128)(2,1)}, u32[]{:S(2)}) copy-start(bf16[15,12,2048]{2,0,1:T(8,128)(2,1)} %param.9) | copy-start | bytes 2211844
  65.9 29.7 %collective-permute-start.5 = (bf16[3,12,512]{2,0,1:T(4,128)(2,1)}, bf16[3,12,512]{2,0,1:T(4,128)(2,1)}, u32[]{:S(2)}, u32[]{:S(2)}) collective-permute-start(bf16[3,12,512]{2,0,1:T(4,128)(2,1)} %copy.54), channel_id=1, source_target_pairs={{1,0},{2,1},{3,2},{4,3},{5,4},{6,5},{7,6},{8,7},{9,8},{10,9},{11,1... | collective-permute-start | bytes 110600 | tf_op jit(solution)/shard_map/ppermute | solution.py:17
  68.1 28.5 %copy-start.56 = (f32[1,512]{1,0:T(1,128)}, f32[1,512]{1,0:T(1,128)S(1)}, u32[]{:S(2)}) copy-start(f32[1,512]{1,0:T(1,128)S(1)} %get-tuple-element.37) | copy-start | bytes 6148
  68.2 25.5 %copy-start.48 = (f32[1,1,512]{2,1,0:T(1,128)}, f32[1,1,512]{2,1,0:T(1,128)S(1)}, u32[]{:S(2)}) copy-start(f32[1,1,512]{2,1,0:T(1,128)S(1)} %get-tuple-element.28) | copy-start | bytes 6148
  68.2 25.5 %copy-start.50 = (f32[1,1,512]{2,1,0:T(1,128)}, f32[1,1,512]{2,1,0:T(1,128)S(1)}, u32[]{:S(2)}) copy-start(f32[1,1,512]{2,1,0:T(1,128)S(1)} %get-tuple-element.29) | copy-start | bytes 6148
  68.2 25.5 %copy-start.52 = (f32[1,1,512]{2,1,0:T(1,128)}, f32[1,1,512]{2,1,0:T(1,128)S(1)}, u32[]{:S(2)}) copy-start(f32[1,1,512]{2,1,0:T(1,128)S(1)} %get-tuple-element.30) | copy-start | bytes 6148
  87.9 5.8 %copy-start.11 = (f32[15,12,512]{2,1,0:T(8,128)S(1)}, f32[15,12,512]{2,1,0:T(8,128)}, u32[]{:S(2)}) copy-start(f32[15,12,512]{2,1,0:T(8,128)} %reshape.954) | copy-start | bytes 1105924
  89.3 6.3 %collective-permute-start.4 = (bf16[3,12,512]{2,0,1:T(4,128)(2,1)S(1)}, bf16[3,12,512]{2,0,1:T(4,128)(2,1)S(1)}, u32[]{:S(2)}, u32[]{:S(2)}) collective-permute-start(bf16[3,12,512]{2,0,1:T(4,128)(2,1)S(1)} %copy-done.39), channel_id=1, source_target_pairs={{0,1},{1,2},{2,3},{3,4},{4,5},{5,6},{6,7},{7,8},{8,9},{9,10},{10,1... | collective-permute-start | bytes 110600 | tf_op jit(solution)/shard_map/ppermute | solution.py:14
  98.1 12.2 %copy-start.7 = (bf16[180,2048]{1,0:T(8,128)(2,1)S(1)}, bf16[180,2048]{1,0:T(8,128)(2,1)}, u32[]{:S(2)}) copy-start(bf16[180,2048]{1,0:T(8,128)(2,1)} %max.13) | copy-start | bytes 2211844
  100.5 17.8 %copy-start = (bf16[2048,512]{1,0:T(8,128)(2,1)S(1)}, bf16[2048,512]{1,0:T(8,128)(2,1)}, u32[]{:S(2)}) copy-start(bf16[2048,512]{1,0:T(8,128)(2,1)} %all-gather.5.cloned.1.call-done) | copy-start | bytes 6291460
  100.5 30.5 %collective-permute-start.3 = (bf16[3,12,512]{2,0,1:T(4,128)(2,1)S(1)}, bf16[3,12,512]{2,0,1:T(4,128)(2,1)S(1)}, u32[]{:S(2)}, u32[]{:S(2)}) collective-permute-start(bf16[3,12,512]{2,0,1:T(4,128)(2,1)S(1)} %copy.49), channel_id=1, source_target_pairs={{1,0},{2,1},{3,2},{4,3},{5,4},{6,5},{7,6},{8,7},{9,8},{10,9},{11,1... | collective-permute-start | bytes 110600 | tf_op jit(solution)/shard_map/ppermute | solution.py:17
  113.1 15.6 %collective-permute-start = (bf16[1,12,512]{2,1,0:T(8,128)(2,1)}, bf16[1,12,512]{2,1,0:T(8,128)(2,1)}, u32[]{:S(2)}, u32[]{:S(2)}) collective-permute-start(bf16[1,12,512]{2,1,0:T(8,128)(2,1)} %get-tuple-element.22), channel_id=1, source_target_pairs={{0,1},{1,2},{2,3},{3,4},{4,5},{5,6},{6,7},{7,8},{8,9},{9,10},{10,1... | collective-permute-start | bytes 36872 | tf_op jit(solution)/shard_map/ppermute | solution.py:14
  116.0 12.6 %collective-permute-start.1 = (bf16[1,12,512]{2,1,0:T(8,128)(2,1)}, bf16[1,12,512]{2,1,0:T(8,128)(2,1)}, u32[]{:S(2)}, u32[]{:S(2)}) collective-permute-start(bf16[1,12,512]{2,1,0:T(8,128)(2,1)} %get-tuple-element.23), channel_id=1, source_target_pairs={{1,0},{2,1},{3,2},{4,3},{5,4},{6,5},{7,6},{8,7},{9,8},{10,9},{11,1... | collective-permute-start | bytes 36872 | tf_op jit(solution)/shard_map/ppermute | solution.py:17
  121.8 9.2 %collective-permute-start.2 = (bf16[3,12,512]{2,0,1:T(4,128)(2,1)S(1)}, bf16[3,12,512]{2,0,1:T(4,128)(2,1)S(1)}, u32[]{:S(2)}, u32[]{:S(2)}) collective-permute-start(bf16[3,12,512]{2,0,1:T(4,128)(2,1)S(1)} %copy.48), channel_id=1, source_target_pairs={{0,1},{1,2},{2,3},{3,4},{4,5},{5,6},{6,7},{7,8},{8,9},{9,10},{10,1... | collective-permute-start | bytes 110600 | tf_op jit(solution)/shard_map/ppermute | solution.py:14
  (50 other events, 121.3 us)
Sparse Core Ops, SparseCore 0:
  10.1 47.4 all-gather.4
  68.1 42.1 all-gather.2
where the time goes:
time: 142 us; the launch traced here: 141 us
  blocking collectives  39.5 us (28%)
  local copies, waits for them, and re-layouts  28.5 us (20%)
  starting transfers between devices  27.8 us (20%)
  between operations  15.2 us (11%)
  other arithmetic  12.5 us (9%)
  matrix products  8.93 us (6%)
  waiting for transfers between devices  8.54 us (6%)
    all_gather x1, blocking collectives, local(): lax.all_gather(square_point, 'rows', axis=0, tiled=True)  22.4 us
    ppermute x5, starting transfers between devices, with_halo(): lax.ppermute(lax.slice_in_dim(block, block.shape[dim] - width, None, axis...  17.5 us
    all_gather x1, blocking collectives, local(): lax.all_gather(column_point, 'rows', axis=0, tiled=True)  17.1 us
    ppermute x5, starting transfers between devices, with_halo(): lax.ppermute(lax.slice_in_dim(block, 0, width, axis=dim), axis, backward)  10.2 us
    unnamed x127, local copies, waits for them, and re-layouts  8.35 us
    all_gather x1, waiting for transfers between devices, local(): lax.all_gather(newer_weight, 'rows', axis=0, tiled=True)  7.82 us
    select_n x2, local copies, waits for them, and re-layouts, local(): older_mask = jnp.where(older_flat > 0, 1.0, 0.0).astype(jnp.float32)  3.64 us
    slice x10, local copies, waits for them, and re-layouts, with_halo(): lax.slice_in_dim(block, block.shape[dim] - width, None, axis=dim)  3.23 us
  transfers between devices with their start and end apart: 12, of which 1 were waited for; matrix products, arithmetic and copies ran while one was open for 31% of the time, Pallas kernels for 0%

commit v1 on v0

--- a/solution.py
+++ b/solution.py
@@ -4,6 +4,11 @@
 from jax.sharding import PartitionSpec as P
 
 HEIGHT = 30
+
+
+def gather_over(x, axis, dim):
+    repeated = jnp.stack([x] * lax.axis_size(axis))
+    return jnp.concatenate(lax.all_to_all(repeated, axis, 0, 0), axis=dim)
 
 
 def with_halo(block, sides, width):
@@ -81,7 +86,7 @@
     older_mixed = older_sum.astype(jnp.bfloat16).reshape(shape_three)
     newer_mixed = newer_sum.astype(jnp.bfloat16).reshape(shape_three)
     square_full, column_full = (
-        lax.all_gather(square_point, "rows", axis=0, tiled=True),
+        gather_over(square_point, "rows", 0),
         lax.all_gather(column_point, "rows", axis=0, tiled=True),
     )
     older_rim = with_halo(older_mixed, (("rows", 0),), 3)

time: 142 us -> 136 us (0.958)
  blocking collectives: 39.5 us -> 23 us
  starting transfers between devices: 27.8 us -> 37.8 us
  local copies, waits for them, and re-layouts: 28.5 us -> 23.2 us
  waiting for transfers between devices: 8.54 us -> 13.1 us
  matrix products: 8.93 us -> 11 us
    all_gather x1 -> x0, blocking collectives: 22.4 us -> none  [local(): lax.all_gather(square_point, 'rows', axis=0, tiled=True)]
    all_to_all x0 -> x1, starting transfers between devices: none -> 10.8 us  [gather_over(): return jnp.concatenate(lax.all_to_all(repeated, axis, 0, 0), axis=dim)]
    all_gather x1, blocking collectives: 17.1 us -> 23 us  [local(): lax.all_gather(column_point, 'rows', axis=0, tiled=True)]
    all_gather x1, waiting for transfers between devices: 7.82 us -> 10.3 us  [local(): lax.all_gather(newer_weight, 'rows', axis=0, tiled=True)]
    unnamed x127 -> x119, local copies, waits for them, and re-layouts: 8.35 us -> 5.9 us
    ppermute x5, waiting for transfers between devices: 0.01 us -> 2.12 us  [with_halo(): lax.ppermute(lax.slice_in_dim(block, 0, width, axis=dim), axis, backward)]
    ppermute x5, starting transfers between devices: 17.5 us -> 15.9 us  [with_halo(): lax.ppermute(lax.slice_in_dim(block, block.shape[dim] - width, None, axis...]
    another operation x0 -> x1, local copies, waits for them, and re-layouts: none -> 1.61 us  [gather_over(): repeated = jnp.stack([x] * lax.axis_size(axis))]
  transfers between devices with their start and end apart: 12 -> 13, of which waited for: 1 -> 2; matrix products, arithmetic and copies ran while one was open for 31% -> 30% of each run, Pallas kernels for 0% -> 0%
where the time goes in v1:
time: 136 us; the launch traced here: 135 us
  starting transfers between devices  37.8 us (28%)
  local copies, waits for them, and re-layouts  23.2 us (17%)
  blocking collectives  23 us (17%)
  between operations  15.2 us (11%)
  waiting for transfers between devices  13.1 us (10%)
  other arithmetic  11.7 us (9%)
  matrix products  11 us (8%)
    all_gather x1, blocking collectives, local(): lax.all_gather(column_point, 'rows', axis=0, tiled=True)  23 us
    ppermute x5, starting transfers between devices, with_halo(): lax.ppermute(lax.slice_in_dim(block, block.shape[dim] - width, None, axis...  15.9 us
    ppermute x5, starting transfers between devices, with_halo(): lax.ppermute(lax.slice_in_dim(block, 0, width, axis=dim), axis, backward)  11 us
    all_to_all x1, starting transfers between devices, gather_over(): return jnp.concatenate(lax.all_to_all(repeated, axis, 0, 0), axis=dim)  10.8 us
    all_gather x1, waiting for transfers between devices, local(): lax.all_gather(newer_weight, 'rows', axis=0, tiled=True)  10.3 us
    unnamed x119, local copies, waits for them, and re-layouts  5.9 us
  transfers between devices with their start and end apart: 13, of which 2 were waited for; matrix products, arithmetic and copies ran while one was open for 30% of the time, Pallas kernels for 0%

profile of v1, /device:TPU:1, one launch (start us, length us, event | category | flops | bytes accessed | tf_op | source)
XLA Modules:
  0.0 135.0 jit_solution(3497305045421964107)
XLA Ops:
  7.9 1.6 %stack.2 = bf16[16,32,512]{2,1,0:T(8,128)(2,1)} broadcast(bf16[32,512]{1,0:T(8,128)(2,1)} %param.14), dimensions={1,2} | broadcast | bytes 557056 | tf_op jit(solution)/shard_map/stack | solution.py:10
  9.5 10.8 %all-to-all-start = ((bf16[16,32,512]{2,1,0:T(8,128)(2,1)}), bf16[16,32,512]{2,1,0:T(8,128)(2,1)}, u32[]{:S(2)}, u32[]{:S(2)}) async-start(bf16[16,32,512]{2,1,0:T(8,128)(2,1)} %stack.2), calls=%async_computation | async-start | bytes 1048576 | tf_op jit(solution)/shard_map/all_to_all | solution.py:11
  21.7 2.3 %collective-permute-start.7 = (bf16[1,12,512]{2,0,1:T(2,128)(2,1)}, bf16[1,12,512]{2,0,1:T(2,128)(2,1)}, u32[]{:S(2)}, u32[]{:S(2)}) collective-permute-start(bf16[1,12,512]{2,0,1:T(2,128)(2,1)} %copy.57), channel_id=1, source_target_pairs={{1,0},{2,1},{3,2},{4,3},{5,4},{6,5},{7,6},{8,7},{9,8},{10,9},{11,1... | collective-permute-start | bytes 36872 | tf_op jit(solution)/shard_map/ppermute | solution.py:22
  24.7 3.5 %collective-permute-start.6 = (bf16[1,12,512]{2,0,1:T(2,128)(2,1)}, bf16[1,12,512]{2,0,1:T(2,128)(2,1)}, u32[]{:S(2)}, u32[]{:S(2)}) collective-permute-start(bf16[1,12,512]{2,0,1:T(2,128)(2,1)} %copy.56), channel_id=1, source_target_pairs={{0,1},{1,2},{2,3},{3,4},{4,5},{5,6},{6,7},{7,8},{8,9},{9,10},{10,1... | collective-permute-start | bytes 36872 | tf_op jit(solution)/shard_map/ppermute | solution.py:19
  28.2 23.0 %all_gather.11 = bf16[512,512]{1,0:T(8,128)(2,1)S(1)} all-gather(bf16[32,512]{1,0:T(8,128)(2,1)S(1)} %copy-done.37), channel_id=1, replica_groups=mesh['dp'=32,'rows'=16] {'rows'}, dimensions={0}, use_global_device_ids=true | all-gather | bytes 557056 | tf_op jit(solution)/shard_map/all_gather | solution.py:90
  53.0 2.1 %collective-permute-start.5 = (bf16[3,12,512]{2,0,1:T(4,128)(2,1)}, bf16[3,12,512]{2,0,1:T(4,128)(2,1)}, u32[]{:S(2)}, u32[]{:S(2)}) collective-permute-start(bf16[3,12,512]{2,0,1:T(4,128)(2,1)} %copy.54), channel_id=1, source_target_pairs={{1,0},{2,1},{3,2},{4,3},{5,4},{6,5},{7,6},{8,7},{9,8},{10,9},{11,1... | collective-permute-start | bytes 110600 | tf_op jit(solution)/shard_map/ppermute | solution.py:22
  55.7 3.5 %collective-permute-start.4 = (bf16[3,12,512]{2,0,1:T(4,128)(2,1)}, bf16[3,12,512]{2,0,1:T(4,128)(2,1)}, u32[]{:S(2)}, u32[]{:S(2)}) collective-permute-start(bf16[3,12,512]{2,0,1:T(4,128)(2,1)} %copy.53), channel_id=1, source_target_pairs={{0,1},{1,2},{2,3},{3,4},{4,5},{5,6},{6,7},{7,8},{8,9},{9,10},{10,1... | collective-permute-start | bytes 110600 | tf_op jit(solution)/shard_map/ppermute | solution.py:19
  63.7 1.3 compare_select_fusion
  72.9 1.4 %select_n.201 = f32[180,2048]{1,0:T(8,128)} reshape(f32[15,12,2048]{2,1,0:T(8,128)S(1)} %copy.60) | data formatting | bytes 2949120 | tf_op jit(solution)/shard_map/jit(_where)/select_n | solution.py:150
  75.7 1.3 select_n.203
  79.0 1.5 %convolution_convert_fusion.2 = bf16[180,512]{1,0:T(8,128)(2,1)S(1)} fusion(bf16[512,512]{1,0:T(8,128)(2,1)} %bitcast.11, bf16[180,2048]{1,0:T(8,128)(2,1)} %copy-done.4), kind=kOutput, calls=%fused_computation.8 | convolution fusion | flops 94464000 | bytes 897024 | tf_op jit(solution)/shard_map/dot_general | solution.py:123
  80.5 1.9 %collective-permute-start.8 = (bf16[1,12,512]{2,1,0:T(8,128)(2,1)S(1)}, bf16[1,12,512]{2,1,0:T(8,128)(2,1)S(1)}, u32[]{:S(2)}, u32[]{:S(2)}) collective-permute-start(bf16[1,12,512]{2,1,0:T(8,128)(2,1)S(1)} %get-tuple-element.18), channel_id=1, source_target_pairs={{0,1},{1,2},{2,3},{3,4},{4,5},{5,6},{6,7},{7,8},{8,9},{9,10},{10,1... | collective-permute-start | bytes 36872 | tf_op jit(solution)/shard_map/ppermute | solution.py:19
  82.4 2.4 %collective-permute-start.9 = (bf16[1,12,512]{2,1,0:T(8,128)(2,1)S(1)}, bf16[1,12,512]{2,1,0:T(8,128)(2,1)S(1)}, u32[]{:S(2)}, u32[]{:S(2)}) collective-permute-start(bf16[1,12,512]{2,1,0:T(8,128)(2,1)S(1)} %get-tuple-element.19), channel_id=1, source_target_pairs={{1,0},{2,1},{3,2},{4,3},{5,4},{6,5},{7,6},{8,7},{9,8},{10,9},{11,1... | collective-permute-start | bytes 36872 | tf_op jit(solution)/shard_map/ppermute | solution.py:22
  85.8 2.1 %collective-permute-done.9 = bf16[1,12,512]{2,1,0:T(8,128)(2,1)S(1)} collective-permute-done((bf16[1,12,512]{2,1,0:T(8,128)(2,1)S(1)}, bf16[1,12,512]{2,1,0:T(8,128)(2,1)S(1)}, u32[]{:S(2)}, u32[]{:S(2)}) %collective-permute-start.9) | collective-permute-done | bytes 12320 | tf_op jit(solution)/shard_map/ppermute | solution.py:22
  89.2 2.2 %convolution_convert_fusion.4 = bf16[180,512]{1,0:T(8,128)(2,1)S(1)} fusion(bf16[180,2048]{1,0:T(8,128)(2,1)S(1)} %copy-done.9, bf16[2048,512]{1,0:T(8,128)(2,1)} %all-gather.5.cloned.1.call-done), kind=kOutput, calls=%fused_computation.10 | convolution fusion | flops 377579520 | bytes 3018752 | tf_op jit(solution)/shard_map/dot_general | solution.py:84
  91.5 2.1 %collective-permute-start.3 = (bf16[3,12,512]{2,0,1:T(4,128)(2,1)S(1)}, bf16[3,12,512]{2,0,1:T(4,128)(2,1)S(1)}, u32[]{:S(2)}, u32[]{:S(2)}) collective-permute-start(bf16[3,12,512]{2,0,1:T(4,128)(2,1)S(1)} %copy.49), channel_id=1, source_target_pairs={{1,0},{2,1},{3,2},{4,3},{5,4},{6,5},{7,6},{8,7},{9,8},{10,9},{11,1... | collective-permute-start | bytes 110600 | tf_op jit(solution)/shard_map/ppermute | solution.py:22
  93.6 10.3 %all-gather.3.cloned.1.call-done = bf16[2048,512]{1,0:T(8,128)(2,1)} async-done(((bf16[128,512]{1,0:T(8,128)(2,1)}), bf16[2048,512]{1,0:T(8,128)(2,1)}) %all-gather.3.cloned.1.call-update) | async-done | bytes 2097168 | tf_op jit(solution)/shard_map/all_gather | solution.py:82
  103.9 2.1 %convolution_convert_fusion.5 = bf16[180,512]{1,0:T(8,128)(2,1)S(1)} fusion(bf16[180,2048]{1,0:T(8,128)(2,1)S(1)} %copy-done.8, bf16[2048,512]{1,0:T(8,128)(2,1)} %all-gather.3.cloned.1.call-done), kind=kOutput, calls=%fused_computation.11 | convolution fusion | flops 377579520 | bytes 3018752 | tf_op jit(solution)/shard_map/dot_general | solution.py:85
  106.6 3.2 %collective-permute-start = (bf16[1,12,512]{2,1,0:T(8,128)(2,1)}, bf16[1,12,512]{2,1,0:T(8,128)(2,1)}, u32[]{:S(2)}, u32[]{:S(2)}) collective-permute-start(bf16[1,12,512]{2,1,0:T(8,128)(2,1)} %get-tuple-element.22), channel_id=1, source_target_pairs={{0,1},{1,2},{2,3},{3,4},{4,5},{5,6},{6,7},{7,8},{8,9},{9,10},{10,1... | collective-permute-start | bytes 36872 | tf_op jit(solution)/shard_map/ppermute | solution.py:19
  109.8 2.2 %collective-permute-start.1 = (bf16[1,12,512]{2,1,0:T(8,128)(2,1)}, bf16[1,12,512]{2,1,0:T(8,128)(2,1)}, u32[]{:S(2)}, u32[]{:S(2)}) collective-permute-start(bf16[1,12,512]{2,1,0:T(8,128)(2,1)} %get-tuple-element.23), channel_id=1, source_target_pairs={{1,0},{2,1},{3,2},{4,3},{5,4},{6,5},{7,6},{8,7},{9,8},{10,9},{11,1... | collective-permute-start | bytes 36872 | tf_op jit(solution)/shard_map/ppermute | solution.py:22
  112.0 2.2 %fusion = bf16[180,2048]{1,0:T(8,128)(2,1)S(1)} fusion(f32[180,2048]{1,0:T(8,128)} %select_n.201, bf16[180,512]{1,0:T(8,128)(2,1)S(1)} %reshape.955, bf16[2048,512]{1,0:T(8,128)(2,1)S(1)} %copy-done), kind=kOutput, calls=%fused_computation.2 | convolution fusion | flops 378224640 | bytes 4493312 | tf_op jit(solution)/shard_map/dot_general | solution.py:152
  115.4 3.8 %collective-permute-start.2 = (bf16[3,12,512]{2,0,1:T(4,128)(2,1)S(1)}, bf16[3,12,512]{2,0,1:T(4,128)(2,1)S(1)}, u32[]{:S(2)}, u32[]{:S(2)}) collective-permute-start(bf16[3,12,512]{2,0,1:T(4,128)(2,1)S(1)} %copy.48), channel_id=1, source_target_pairs={{0,1},{1,2},{2,3},{3,4},{4,5},{5,6},{6,7},{7,8},{8,9},{9,10},{10,1... | collective-permute-start | bytes 110600 | tf_op jit(solution)/shard_map/ppermute | solution.py:19
  119.5 1.3 copy.62
  123.7 1.3 convolution_convert_fusion.1
  (198 shorter events, 30.5 us)
Async XLA Ops:
  7.2 13.2 %copy-start.15 = (bf16[15,12,2048]{2,0,1:T(8,128)(2,1)S(1)}, bf16[15,12,2048]{2,0,1:T(8,128)(2,1)}, u32[]{:S(2)}) copy-start(bf16[15,12,2048]{2,0,1:T(8,128)(2,1)} %param.11) | copy-start | bytes 2211844
  7.2 82.1 %all-gather.5.cloned.1.call-start = ((), (), s32[]{:S(2)}) async-start(), calls=%async_computation.2 | async-start | bytes 2228224 | tf_op jit(solution)/shard_map/all_gather | solution.py:81
  9.5 69.4 %all-to-all-start = ((bf16[16,32,512]{2,1,0:T(8,128)(2,1)}), bf16[16,32,512]{2,1,0:T(8,128)(2,1)}, u32[]{:S(2)}, u32[]{:S(2)}) async-start(bf16[16,32,512]{2,1,0:T(8,128)(2,1)} %stack.2), calls=%async_computation | async-start | bytes 1048576 | tf_op jit(solution)/shard_map/all_to_all | solution.py:11
  20.3 83.5 %all-gather.3.cloned.1.call-start = ((), (), s32[]{:S(2)}) async-start(), calls=%async_computation.1 | async-start | bytes 2228224 | tf_op jit(solution)/shard_map/all_gather | solution.py:82
  21.0 39.1 %copy-start.4 = (bf16[180,2048]{1,0:T(8,128)(2,1)}, bf16[180,2048]{1,0:T(8,128)(2,1)S(1)}, u32[]{:S(2)}) copy-start(bf16[180,2048]{1,0:T(8,128)(2,1)S(1)} %reshape.952) | copy-start | bytes 2211844
  21.7 38.4 %copy-start.51 = (f32[7,512]{1,0:T(8,128)S(1)}, f32[7,512]{1,0:T(8,128)}, u32[]{:S(2)}) copy-start(f32[7,512]{1,0:T(8,128)} %param.17) | copy-start | bytes 43012
  21.7 55.4 %collective-permute-start.7 = (bf16[1,12,512]{2,0,1:T(2,128)(2,1)}, bf16[1,12,512]{2,0,1:T(2,128)(2,1)}, u32[]{:S(2)}, u32[]{:S(2)}) collective-permute-start(bf16[1,12,512]{2,0,1:T(2,128)(2,1)} %copy.57), channel_id=1, source_target_pairs={{1,0},{2,1},{3,2},{4,3},{5,4},{6,5},{7,6},{8,7},{9,8},{10,9},{11,1... | collective-permute-start | bytes 36872 | tf_op jit(solution)/shard_map/ppermute | solution.py:22
  24.0 36.1 %copy-start.50 = (f32[3,3,512]{2,1,0:T(4,128)S(1)}, f32[3,3,512]{2,1,0:T(4,128)}, u32[]{:S(2)}) copy-start(f32[3,3,512]{2,1,0:T(4,128)} %param.16) | copy-start | bytes 55300
  24.7 35.5 %copy-start.6 = (bf16[15,12,2048]{2,0,1:T(8,128)(2,1)S(1)}, bf16[15,12,2048]{2,0,1:T(8,128)(2,1)}, u32[]{:S(2)}) copy-start(bf16[15,12,2048]{2,0,1:T(8,128)(2,1)} %param.9) | copy-start | bytes 2211844
  24.7 52.4 %collective-permute-start.6 = (bf16[1,12,512]{2,0,1:T(2,128)(2,1)}, bf16[1,12,512]{2,0,1:T(2,128)(2,1)}, u32[]{:S(2)}, u32[]{:S(2)}) collective-permute-start(bf16[1,12,512]{2,0,1:T(2,128)(2,1)} %copy.56), channel_id=1, source_target_pairs={{0,1},{1,2},{2,3},{3,4},{4,5},{5,6},{6,7},{7,8},{8,9},{9,10},{10,1... | collective-permute-start | bytes 36872 | tf_op jit(solution)/shard_map/ppermute | solution.py:19
  53.0 25.0 %collective-permute-start.5 = (bf16[3,12,512]{2,0,1:T(4,128)(2,1)}, bf16[3,12,512]{2,0,1:T(4,128)(2,1)}, u32[]{:S(2)}, u32[]{:S(2)}) collective-permute-start(bf16[3,12,512]{2,0,1:T(4,128)(2,1)} %copy.54), channel_id=1, source_target_pairs={{1,0},{2,1},{3,2},{4,3},{5,4},{6,5},{7,6},{8,7},{9,8},{10,9},{11,1... | collective-permute-start | bytes 110600 | tf_op jit(solution)/shard_map/ppermute | solution.py:22
  55.7 22.3 %collective-permute-start.4 = (bf16[3,12,512]{2,0,1:T(4,128)(2,1)}, bf16[3,12,512]{2,0,1:T(4,128)(2,1)}, u32[]{:S(2)}, u32[]{:S(2)}) collective-permute-start(bf16[3,12,512]{2,0,1:T(4,128)(2,1)} %copy.53), channel_id=1, source_target_pairs={{0,1},{1,2},{2,3},{3,4},{4,5},{5,6},{6,7},{7,8},{8,9},{9,10},{10,1... | collective-permute-start | bytes 110600 | tf_op jit(solution)/shard_map/ppermute | solution.py:19
  60.1 24.7 %copy-start.52 = (f32[1,512]{1,0:T(1,128)}, f32[1,512]{1,0:T(1,128)S(1)}, u32[]{:S(2)}) copy-start(f32[1,512]{1,0:T(1,128)S(1)} %get-tuple-element.37) | copy-start | bytes 6148
  60.1 27.8 %copy-start.44 = (f32[1,1,512]{2,1,0:T(1,128)}, f32[1,1,512]{2,1,0:T(1,128)S(1)}, u32[]{:S(2)}) copy-start(f32[1,1,512]{2,1,0:T(1,128)S(1)} %get-tuple-element.28) | copy-start | bytes 6148
  60.2 27.8 %copy-start.46 = (f32[1,1,512]{2,1,0:T(1,128)}, f32[1,1,512]{2,1,0:T(1,128)S(1)}, u32[]{:S(2)}) copy-start(f32[1,1,512]{2,1,0:T(1,128)S(1)} %get-tuple-element.29) | copy-start | bytes 6148
  60.2 27.8 %copy-start.48 = (f32[1,1,512]{2,1,0:T(1,128)}, f32[1,1,512]{2,1,0:T(1,128)S(1)}, u32[]{:S(2)}) copy-start(f32[1,1,512]{2,1,0:T(1,128)S(1)} %get-tuple-element.30) | copy-start | bytes 6148
  80.5 5.3 %collective-permute-start.8 = (bf16[1,12,512]{2,1,0:T(8,128)(2,1)S(1)}, bf16[1,12,512]{2,1,0:T(8,128)(2,1)S(1)}, u32[]{:S(2)}, u32[]{:S(2)}) collective-permute-start(bf16[1,12,512]{2,1,0:T(8,128)(2,1)S(1)} %get-tuple-element.18), channel_id=1, source_target_pairs={{0,1},{1,2},{2,3},{3,4},{4,5},{5,6},{6,7},{7,8},{8,9},{9,10},{10,1... | collective-permute-start | bytes 36872 | tf_op jit(solution)/shard_map/ppermute | solution.py:19
  82.4 5.5 %collective-permute-start.9 = (bf16[1,12,512]{2,1,0:T(8,128)(2,1)S(1)}, bf16[1,12,512]{2,1,0:T(8,128)(2,1)S(1)}, u32[]{:S(2)}, u32[]{:S(2)}) collective-permute-start(bf16[1,12,512]{2,1,0:T(8,128)(2,1)S(1)} %get-tuple-element.19), channel_id=1, source_target_pairs={{1,0},{2,1},{3,2},{4,3},{5,4},{6,5},{7,6},{8,7},{9,8},{10,9},{11,1... | collective-permute-start | bytes 36872 | tf_op jit(solution)/shard_map/ppermute | solution.py:22
  89.2 14.6 %copy-start.8 = (bf16[180,2048]{1,0:T(8,128)(2,1)S(1)}, bf16[180,2048]{1,0:T(8,128)(2,1)}, u32[]{:S(2)}) copy-start(bf16[180,2048]{1,0:T(8,128)(2,1)} %max.13) | copy-start | bytes 2211844
  91.5 20.5 %copy-start = (bf16[2048,512]{1,0:T(8,128)(2,1)S(1)}, bf16[2048,512]{1,0:T(8,128)(2,1)}, u32[]{:S(2)}) copy-start(bf16[2048,512]{1,0:T(8,128)(2,1)} %all-gather.5.cloned.1.call-done) | copy-start | bytes 6291460
  91.5 33.5 %collective-permute-start.3 = (bf16[3,12,512]{2,0,1:T(4,128)(2,1)S(1)}, bf16[3,12,512]{2,0,1:T(4,128)(2,1)S(1)}, u32[]{:S(2)}, u32[]{:S(2)}) collective-permute-start(bf16[3,12,512]{2,0,1:T(4,128)(2,1)S(1)} %copy.49), channel_id=1, source_target_pairs={{1,0},{2,1},{3,2},{4,3},{5,4},{6,5},{7,6},{8,7},{9,8},{10,9},{11,1... | collective-permute-start | bytes 110600 | tf_op jit(solution)/shard_map/ppermute | solution.py:22
  106.6 15.7 %collective-permute-start = (bf16[1,12,512]{2,1,0:T(8,128)(2,1)}, bf16[1,12,512]{2,1,0:T(8,128)(2,1)}, u32[]{:S(2)}, u32[]{:S(2)}) collective-permute-start(bf16[1,12,512]{2,1,0:T(8,128)(2,1)} %get-tuple-element.22), channel_id=1, source_target_pairs={{0,1},{1,2},{2,3},{3,4},{4,5},{5,6},{6,7},{7,8},{8,9},{9,10},{10,1... | collective-permute-start | bytes 36872 | tf_op jit(solution)/shard_map/ppermute | solution.py:19
  109.8 12.5 %collective-permute-start.1 = (bf16[1,12,512]{2,1,0:T(8,128)(2,1)}, bf16[1,12,512]{2,1,0:T(8,128)(2,1)}, u32[]{:S(2)}, u32[]{:S(2)}) collective-permute-start(bf16[1,12,512]{2,1,0:T(8,128)(2,1)} %get-tuple-element.23), channel_id=1, source_target_pairs={{1,0},{2,1},{3,2},{4,3},{5,4},{6,5},{7,6},{8,7},{9,8},{10,9},{11,1... | collective-permute-start | bytes 36872 | tf_op jit(solution)/shard_map/ppermute | solution.py:22
  115.4 9.6 %collective-permute-start.2 = (bf16[3,12,512]{2,0,1:T(4,128)(2,1)S(1)}, bf16[3,12,512]{2,0,1:T(4,128)(2,1)S(1)}, u32[]{:S(2)}, u32[]{:S(2)}) collective-permute-start(bf16[3,12,512]{2,0,1:T(4,128)(2,1)S(1)} %copy.48), channel_id=1, source_target_pairs={{0,1},{1,2},{2,3},{3,4},{4,5},{5,6},{6,7},{7,8},{8,9},{9,10},{10,1... | collective-permute-start | bytes 110600 | tf_op jit(solution)/shard_map/ppermute | solution.py:19
  (47 other events, 145.8 us)
Sparse Core Ops, SparseCore 0:
  10.1 49.7 all-gather.4
  62.0 41.8 all-gather.2
